TPU v7x, 32 devices: a whole 2x2x4 slice. The times are simulated.
32 devices in a mesh: rows: 8 (over z, y), grp: 4 (over x, core).
Axes of the slice: x: 2, y: 2, z: 4, core: 2. Of those that a mesh axis runs over, the one named last changes fastest.
Arguments:
- a_vals: bfloat16 [2048, 16384], P(('rows', 'grp')), may hold values from -0.75 to 0.75
- a_cols: int32 [2048, 4], P(('rows', 'grp')), may hold values from 0 to 2047, as said below
- p_vals: bfloat16 [2048, 16384], P(('rows', 'grp')), may hold values from -0.25 to 0.25
- new_rows: int32 [2048], P(('rows', 'grp')), may hold values from 0 to 7, as said below
Outputs:
- a_moved: bfloat16 [2048, 16384], P(('rows', 'grp'))
- coarse: bfloat16 [2048, 768], P(('rows', 'grp'))
Inputs may be any that keep to these rules, and one draw needn't show every extreme that they name: `a_cols`: the first entry of row i is i itself; every entry names a block row whose slab is slab(i) - 1, slab(i) or slab(i) + 1, with any grp index. `new_rows`: the rows of one device go to each rows index either none or exactly 16 at a time, and for each grp index every rows index receives exactly 64 rows.
All inputs are finite; a program needn't handle non-finite values.
Results may differ from a plain program's by a relative error of at most 0.005.
Values may be sent and summed in bfloat16 or wider, within the bound.
No kernel may reach another device: no remote copies, remote signals or barrier semaphores. Data moves between devices by JAX's collectives and lax.ppermute only.
A program may use at most 192 MiB of HBM per device.

v0:
```python
import jax
import jax.numpy as jnp
from jax import lax
from jax.sharding import PartitionSpec as P

B = 64


def extended(block, sides, width):
    for axis, dim in sides:
        count = lax.axis_size(axis)
        forward = [(i, i + 1) for i in range(count - 1)]
        backward = [(target, source) for source, target in forward]
        low = lax.ppermute(
            lax.slice_in_dim(block, block.shape[dim] - width, None, axis=dim), axis, forward
        )
        high = lax.ppermute(lax.slice_in_dim(block, 0, width, axis=dim), axis, backward)
        block = jnp.concatenate([low, block, high], axis=dim)
    return block


def select_rows(picker, source):
    return jnp.dot(picker, source, preferred_element_type=jnp.float32).astype(jnp.bfloat16)


def migrate(a_vals, new_rows):
    row_count, row_width = a_vals.shape
    rows_total = lax.axis_size("rows")
    capacity = max(2, 2 * row_count // rows_total)
    slot_total = rows_total * capacity
    dest_hot = (new_rows[:, None] == jnp.arange(rows_total, dtype=jnp.int32)[None, :]).astype(
        jnp.int32
    )
    ranking = jnp.sum((jnp.cumsum(dest_hot, axis=0) - 1) * dest_hot, axis=1)
    slot_of = new_rows * capacity + ranking
    slot_ids = jnp.arange(slot_total, dtype=jnp.int32)
    sender = (slot_ids[:, None] == slot_of[None, :]).astype(jnp.bfloat16)
    outgoing = select_rows(sender, a_vals)
    filled = jnp.sum(sender, axis=1)
    incoming, flags = (
        lax.all_to_all(
            outgoing.reshape(rows_total, capacity, row_width),
            "rows",
            split_axis=0,
            concat_axis=0,
            tiled=True,
        ),
        lax.all_to_all(
            filled.reshape(rows_total, capacity), "rows", split_axis=0, concat_axis=0, tiled=True
        ),
    )
    flat_flags = flags.reshape(slot_total).astype(jnp.float32)
    position = jnp.cumsum(flat_flags) - 1.0
    flat_rows = incoming.reshape(slot_total, row_width)
    wanted = jnp.arange(row_count, dtype=jnp.float32)
    receiver = ((position[None, :] == wanted[:, None]) & (flat_flags[None, :] > 0.0)).astype(
        jnp.bfloat16
    )
    return select_rows(receiver, flat_rows)


def galerkin(a_vals, a_cols, p_vals):
    row_count, band = a_cols.shape
    slab_width = p_vals.shape[1] // B
    rows_pos = lax.axis_index("rows")
    slab_rows = row_count * lax.axis_size("grp")
    slab_all = lax.all_gather(p_vals, "grp", axis=0, tiled=True)
    padded = extended(slab_all, (("rows", 0),), slab_rows)
    owner_slab = a_cols // slab_rows
    window_slot = owner_slab - rows_pos + 1
    local_row = window_slot * slab_rows + (a_cols - owner_slab * slab_rows)
    gathered = padded[local_row].reshape(row_count, band, B, slab_width)
    blocks = a_vals.reshape(row_count, B, band, B)
    pieces = []
    for offset in range(3):
        kept_mask = (window_slot == offset).astype(jnp.bfloat16)
        masked = blocks * kept_mask[:, None, :, None]
        pieces.append(
            jnp.einsum("jake,jkef->jaf", masked, gathered, preferred_element_type=jnp.float32)
        )
    products = jnp.stack(pieces, axis=2).reshape(row_count * B, 3 * slab_width).astype(jnp.bfloat16)
    own_rows = p_vals.reshape(row_count * B, slab_width)
    partial_sum = lax.dot_general(
        own_rows, products, (((0,), (0,)), ((), ())), preferred_element_type=jnp.float32
    )
    return lax.psum_scatter(partial_sum, "grp", scatter_dimension=0, tiled=True).astype(
        jnp.bfloat16
    )


def local(a_vals, a_cols, p_vals, new_rows):
    coarse = galerkin(a_vals, a_cols, p_vals)
    a_moved = migrate(a_vals, new_rows)
    return (a_moved, coarse)


def solution(mesh):
    in_specs = (
        P(("rows", "grp"), None),
        P(("rows", "grp"), None),
        P(("rows", "grp"), None),
        P(("rows", "grp")),
    )
    out_specs = (P(("rows", "grp"), None), P(("rows", "grp"), None))
    return jax.shard_map(local, mesh=mesh, in_specs=in_specs, out_specs=out_specs, check_vma=False)
```

profile of v0, /device:TPU:0, one launch (start us, length us, event | category | flops | bytes accessed | tf_op | source)
XLA Modules:
  0.0 567.7 jit_solution(2155070878512227861)
XLA Ops:
  7.2 0.0 all-gather.2.cloned.1.call-start
  7.2 0.7 all-gather.2.cloned.1.call-update
  7.9 62.6 %all-gather.2.cloned.1.call-done = bf16[256,16384]{1,0:T(8,128)(2,1)} async-done(((bf16[64,16384]{1,0:T(8,128)(2,1)}), bf16[256,16384]{1,0:T(8,128)(2,1)}) %all-gather.2.cloned.1.call-update) | async-done | bytes 8388624 | tf_op jit(solution)/shard_map/all_gather | solution.py:67
  70.5 6.6 %collective-permute-start = (bf16[256,16384]{1,0:T(8,128)(2,1)}, bf16[256,16384]{1,0:T(8,128)(2,1)}, u32[]{:S(2)}, u32[]{:S(2)}) collective-permute-start(bf16[256,16384]{1,0:T(8,128)(2,1)} %all-gather.2.cloned.1.call-done), channel_id=1, source_target_pairs={{0,4},{4,8},{8,12},{12,16},{16,20},{20,24},{24,28},{1,5},{5,9},{9,... | collective-permute-start | bytes 25165832 | tf_op jit(solution)/shard_map/ppermute | solution.py:14
  77.1 1.3 collective-permute-start.1
  78.4 0.7 fusion.21
  79.1 0.1 reduce_window_sum.18
  79.2 0.8 select_reduce_fusion
  80.1 0.7 multiply_add_fusion
  80.7 0.1 fusion.25
  80.8 0.7 all_to_all.12
  81.5 6.7 %all-to-all-start = ((bf16[8,1,16]{2,1,0:T(2,128)(2,1)}), bf16[8,1,16]{2,1,0:T(2,128)(2,1)S(1)}, u32[]{:S(2)}, u32[]{:S(2)}) async-start(bf16[8,1,16]{2,1,0:T(2,128)(2,1)} %all_to_all.12), calls=%async_computation | async-start | bytes 8192 | tf_op jit(solution)/shard_map/all_to_all | solution.py:48
  88.2 0.7 compare_convert_fusion.2
  88.9 0.7 compare_select_fusion
  89.6 4.9 convolution_convert_fusion
  94.5 0.1 copy.50
  94.6 0.1 reshape.92
  94.7 339.4 %all-to-all-done = bf16[8,1,16]{2,1,0:T(2,128)(2,1)S(1)} async-done(((bf16[8,1,16]{2,1,0:T(2,128)(2,1)}), bf16[8,1,16]{2,1,0:T(2,128)(2,1)S(1)}, u32[]{:S(2)}, u32[]{:S(2)}) %all-to-all-start) | async-done | bytes 288 | tf_op jit(solution)/shard_map/all_to_all | solution.py:48
  434.2 6.6 %all-to-all-start.1 = ((bf16[8,16,16384]{2,1,0:T(8,128)(2,1)}), bf16[8,16,16384]{2,1,0:T(8,128)(2,1)}, u32[]{:S(2)}, u32[]{:S(2)}) async-start(bf16[8,16,16384]{2,1,0:T(8,128)(2,1)} %bitcast.42), calls=%async_computation.1 | async-start | bytes 8388608 | tf_op jit(solution)/shard_map/all_to_all | solution.py:41
  440.8 0.0 reduce-scatter.4.cloned.1.call-start
  440.9 5.5 reshape.86
  446.4 2.9 reshape.88
  449.3 0.1 copy.51
  449.4 0.1 copy.53
  449.5 0.1 copy.48
  449.6 0.0 collective-permute-done
  449.6 17.6 %pad_maximum_fusion = bf16[768,16384]{1,0:T(8,128)(2,1)} fusion(bf16[256,16384]{1,0:T(8,128)(2,1)} %collective-permute-done.1, bf16[256,16384]{1,0:T(8,128)(2,1)} %all-gather.2.cloned.1.call-done, bf16[256,16384]{1,0:T(8,128)(2,1)} %collective-permute-done), kind=kLoop, calls=%fused_computation.1 | loop fusion | flops 75497472 | bytes 50331648 | tf_op jit(solution)/shard_map/concatenate | solution.py:18
  467.3 22.2 %gather_fusion = bf16[256,16384]{1,0:T(8,128)(2,1)} fusion(bf16[768,16384]{1,0:T(8,128)(2,1)} %pad_maximum_fusion, s32[1024]{0:T(1024)S(1)} %pad_clamp_fusion), kind=kCustom, calls=%fused_computation | custom fusion | bytes 16778240 | tf_op jit(solution)/shard_map/gather | solution.py:72
  489.4 9.4 %copy.62 = bf16[32,8,64,256]{3,2,1,0:T(8,128)(2,1)} copy(bf16[32,8,64,256]{3,1,2,0:T(8,128)(2,1)} %bitcast.39) | data formatting | bytes 16777216
  498.8 6.7 %fusion.10 = bf16[64,64,1,256]{3,1,0,2:T(8,128)(2,1)S(1)} fusion(bf16[64,4,64,256]{3,2,1,0:T(8,128)(2,1)} %bitcast.43, bf16[64,64,4,64]{3,2,1,0:T(4,128)(2,1)} %reshape.86, bf16[64,4]{1,0:T(8,128)(2,1)S(1)} %copy.51), kind=kOutput, calls=%fused_computation.18 | convolution fusion | flops 538968064 | bytes 12583424 | tf_op jit(solution)/shard_map/jake,jkef->jaf/dot_general | solution.py:79
  505.6 0.3 copy-done.1
  505.9 1.2 copy-done.2
  507.0 2.2 fusion.11
  509.3 2.2 fusion.9
  511.5 3.1 pad_maximum_fusion.1
  514.7 12.3 %copy.55 = bf16[64,64,3,256]{3,2,1,0:T(4,128)(2,1)} copy(bf16[64,64,3,256]{3,1,0,2:T(8,128)(2,1)} %pad_maximum_fusion.1) | data formatting | bytes 12582912 | tf_op jit(solution)/shard_map/stack | solution.py:81
  527.0 5.2 copy.63
  532.2 1.8 convolution_bitcast_fusion
  534.0 1.1 copy.60
  535.2 0.0 reduce-scatter.4.cloned.1.call-update
  535.2 0.1 reshape.104
  535.4 0.1 gt.16
  535.4 0.2 reduce-window.8
  535.6 0.1 add_reduce_fusion
  535.7 4.2 convolution_convert_fusion.1
  539.9 19.1 %reduce-scatter.4.cloned.1.call-done = f32[64,768]{1,0:T(8,128)} async-done(((f32[256,768]{1,0:T(8,128)}), f32[64,768]{1,0:T(8,128)}) %reduce-scatter.4.cloned.1.call-update) | async-done | bytes 196624
  559.0 1.1 copy.61
  560.1 0.8 copy.56
  (10 shorter events, 0.1 us)
Async XLA Ops:
  7.2 63.4 %all-gather.2.cloned.1.call-start = ((), (), s32[]{:S(2)}) async-start(), calls=%async_computation.3 | async-start | bytes 10485760 | tf_op jit(solution)/shard_map/all_gather | solution.py:67
  70.5 379.1 %collective-permute-start = (bf16[256,16384]{1,0:T(8,128)(2,1)}, bf16[256,16384]{1,0:T(8,128)(2,1)}, u32[]{:S(2)}, u32[]{:S(2)}) collective-permute-start(bf16[256,16384]{1,0:T(8,128)(2,1)} %all-gather.2.cloned.1.call-done), channel_id=1, source_target_pairs={{0,4},{4,8},{8,12},{12,16},{16,20},{20,24},{24,28},{1,5},{5,9},{9,... | collective-permute-start | bytes 25165832 | tf_op jit(solution)/shard_map/ppermute | solution.py:14
  77.1 372.5 %collective-permute-start.1 = (bf16[256,16384]{1,0:T(8,128)(2,1)}, bf16[256,16384]{1,0:T(8,128)(2,1)}, u32[]{:S(2)}, u32[]{:S(2)}) collective-permute-start(bf16[256,16384]{1,0:T(8,128)(2,1)} %all-gather.2.cloned.1.call-done), channel_id=1, source_target_pairs={{4,0},{8,4},{12,8},{16,12},{20,16},{24,20},{28,24},{5,1},{9,5},{13... | collective-permute-start | bytes 25165832 | tf_op jit(solution)/shard_map/ppermute | solution.py:17
  81.5 352.6 %all-to-all-start = ((bf16[8,1,16]{2,1,0:T(2,128)(2,1)}), bf16[8,1,16]{2,1,0:T(2,128)(2,1)S(1)}, u32[]{:S(2)}, u32[]{:S(2)}) async-start(bf16[8,1,16]{2,1,0:T(2,128)(2,1)} %all_to_all.12), calls=%async_computation | async-start | bytes 8192 | tf_op jit(solution)/shard_map/all_to_all | solution.py:48
  434.2 6.7 %copy-start = (bf16[64,16384]{1,0:T(8,128)(2,1)S(1)}, bf16[64,16384]{1,0:T(8,128)(2,1)}, u32[]{:S(2)}) copy-start(bf16[64,16384]{1,0:T(8,128)(2,1)} %param.4) | copy-start | bytes 6291460
  434.2 101.6 %all-to-all-start.1 = ((bf16[8,16,16384]{2,1,0:T(8,128)(2,1)}), bf16[8,16,16384]{2,1,0:T(8,128)(2,1)}, u32[]{:S(2)}, u32[]{:S(2)}) async-start(bf16[8,16,16384]{2,1,0:T(8,128)(2,1)} %bitcast.42), calls=%async_computation.1 | async-start | bytes 8388608 | tf_op jit(solution)/shard_map/all_to_all | solution.py:41
  440.8 118.2 %reduce-scatter.4.cloned.1.call-start = ((), (), s32[]{:S(2)}) async-start(), calls=%async_computation.4 | async-start | bytes 983040
  498.8 7.0 %copy-start.1 = (bf16[32,8,64,256]{3,2,1,0:T(8,128)(2,1)S(1)}, bf16[32,8,64,256]{3,2,1,0:T(8,128)(2,1)}, u32[]{:S(2)}) copy-start(bf16[32,8,64,256]{3,2,1,0:T(8,128)(2,1)} %copy.62) | copy-start | bytes 25165828
  498.8 8.2 %copy-start.2 = (bf16[64,64,4,64]{3,2,1,0:T(4,128)(2,1)S(1)}, bf16[64,64,4,64]{3,2,1,0:T(4,128)(2,1)}, u32[]{:S(2)}) copy-start(bf16[64,64,4,64]{3,2,1,0:T(4,128)(2,1)} %reshape.86) | copy-start | bytes 6291460
Sparse Core Ops, SparseCore 0:
  9.5 60.9 all-gather.1
  535.3 23.6 reduce-scatter.3
where the time goes:
time: 568 us
  waiting for transfers between devices  422 us (74%)
  local copies, waits for them, and re-layouts  63.4 us (11%)
  other arithmetic  24.9 us (4%)
  matrix products  22.1 us (4%)
  starting transfers between devices  21.3 us (4%)
  between operations  14.2 us (2%)
    all_to_all x1, waiting for transfers between devices, migrate(): lax.all_to_all(filled.reshape(rows_total, capacity), 'rows', split_axis=0...  339 us
    all_gather x1, waiting for transfers between devices, galerkin(): slab_all = lax.all_gather(p_vals, 'grp', axis=0, tiled=True)  62.6 us
    gather x1, local copies, waits for them, and re-layouts, galerkin(): gathered = padded[local_row].reshape(row_count, band, B, slab_width)  22.2 us
    unnamed x3, waiting for transfers between devices  19.8 us
    unnamed x11, local copies, waits for them, and re-layouts  19.1 us
    concatenate x1, other arithmetic, extended(): block = jnp.concatenate([low, block, high], axis=dim)  17.6 us
    another operation x1, local copies, waits for them, and re-layouts, galerkin(): jnp.stack(pieces, axis=2).reshape(row_count * B, 3 * slab_width)  12.3 us
  transfers between devices with their start and end apart: 6, of which 3 were waited for; matrix products, arithmetic and copies ran while one was open for 19% of the time, Pallas kernels for 0%

commit v1 on v0

--- a/solution.py
+++ b/solution.py
@@ -4,6 +4,32 @@
 from jax.sharding import PartitionSpec as P
 
 B = 64
+
+
+def view_stacks_all_on_mesh(unit, dimension_no):
+    unit = jnp.moveaxis(unit, 0, dimension_no)
+    after = unit.shape
+    return unit.reshape(
+        *after[:dimension_no],
+        after[dimension_no] * after[dimension_no + 1],
+        *after[dimension_no + 2 :]
+    )
+
+
+def row_get(inp, net_axis):
+    axis_n = lax.axis_size(net_axis)
+    big = inp[None]
+    for idx in range(axis_n.bit_length() - 1):
+        y_new = 1 << idx
+        x_new = range(axis_n)
+        clean = map(lambda dev: (dev, dev ^ y_new), x_new)
+        extra = list(clean)
+        ready = lax.ppermute(big, axis_name=net_axis, perm=extra)
+        outer = jnp.stack([big, ready])
+        current_arr = lax.axis_index(net_axis)
+        inter = current_arr >> idx & 1
+        big = jnp.where(inter == 0, outer, outer[::-1]).reshape(-1, *inp.shape)
+    return big
 
 
 def extended(block, sides, width):
@@ -64,7 +90,8 @@
     slab_width = p_vals.shape[1] // B
     rows_pos = lax.axis_index("rows")
     slab_rows = row_count * lax.axis_size("grp")
-    slab_all = lax.all_gather(p_vals, "grp", axis=0, tiled=True)
+    last = row_get(p_vals, "grp")
+    slab_all = view_stacks_all_on_mesh(last, 0)
     padded = extended(slab_all, (("rows", 0),), slab_rows)
     owner_slab = a_cols // slab_rows
     window_slot = owner_slab - rows_pos + 1

time: 568 us -> 636 us (1.12)
  waiting for transfers between devices: 422 us -> 458 us
  other arithmetic: 24.9 us -> 47.8 us
    ppermute x0 -> x2, waiting for transfers between devices: none -> 95.2 us  [row_get(): ready = lax.ppermute(big, axis_name=net_axis, perm=extra)]
    all_gather x1 -> x0, waiting for transfers between devices: 62.6 us -> none  [galerkin(): slab_all = lax.all_gather(p_vals, 'grp', axis=0, tiled=True)]
    another operation x1 -> x4, other arithmetic: 0.17 us -> 13.9 us  [the longest x3 13.7 us: row_get(): outer = jnp.stack([big, ready])]
    select_n x0 -> x1, other arithmetic: none -> 12.3 us  [row_get(): big = jnp.where(inter == 0, outer, outer[::-1]).reshape(-1, *inp.shape)]
    unnamed x3 -> x2, waiting for transfers between devices: 19.8 us -> 20 us
    unnamed x11 -> x15, local copies, waits for them, and re-layouts: 19.1 us -> 19.1 us
  transfers between devices with their start and end apart: 6 -> 7, of which waited for: 3 -> 4; matrix products, arithmetic and copies ran while one was open for 19% -> 16% of each run, Pallas kernels for 0% -> 0%
where the time goes in v1:
time: 636 us; the launch traced here: 630 us
  waiting for transfers between devices  458 us (72%)
  local copies, waits for them, and re-layouts  63.6 us (10%)
  other arithmetic  47.8 us (8%)
  starting transfers between devices  25.8 us (4%)
  matrix products  20.5 us (3%)
  between operations  14.4 us (2%)
    all_to_all x1, waiting for transfers between devices, migrate(): lax.all_to_all(filled.reshape(rows_total, capacity), 'rows', split_axis=0...  343 us
    ppermute x2, waiting for transfers between devices, row_get(): ready = lax.ppermute(big, axis_name=net_axis, perm=extra)  95.2 us
    gather x1, local copies, waits for them, and re-layouts, galerkin(): gathered = padded[local_row].reshape(row_count, band, B, slab_width)  22.3 us
    unnamed x2, waiting for transfers between devices  20 us
    unnamed x15, local copies, waits for them, and re-layouts  19.1 us
    concatenate x1, other arithmetic, extended(): block = jnp.concatenate([low, block, high], axis=dim)  17.6 us
    another operation x3, other arithmetic, row_get(): outer = jnp.stack([big, ready])  13.7 us
  transfers between devices with their start and end apart: 7, of which 4 were waited for; matrix products, arithmetic and copies ran while one was open for 16% of the time, Pallas kernels for 0%

profile of v1, /device:TPU:0, one launch (start us, length us, event | category | flops | bytes accessed | tf_op | source)
XLA Modules:
  0.0 630.4 jit_solution(4027422215682709605)
XLA Ops:
  7.2 0.6 collective-permute-start
  7.7 4.0 collective-permute-done
  11.7 2.0 pad_maximum_fusion.3
  13.7 4.3 fusion.10
  18.0 2.8 collective-permute-start.1
  20.8 91.2 %collective-permute-done.1 = bf16[2,64,16384]{2,1,0:T(8,128)(2,1)} collective-permute-done((bf16[2,64,16384]{2,1,0:T(8,128)(2,1)}, bf16[2,64,16384]{2,1,0:T(8,128)(2,1)}, u32[]{:S(2)}, u32[]{:S(2)}) %collective-permute-start.1) | collective-permute-done | bytes 4194336 | tf_op jit(solution)/shard_map/ppermute | solution.py:27
  112.0 7.5 %pad_maximum_fusion.1 = bf16[2,2,64,16384]{3,2,1,0:T(8,128)(2,1)} fusion(bf16[1,2,64,16384]{3,2,1,0:T(8,128)(2,1)} %bitcast.7, bf16[1,2,64,16384]{3,2,1,0:T(8,128)(2,1)} %get-tuple-element.14), kind=kLoop, calls=%fused_computation.5 | loop fusion | flops 4194304 | bytes 16777216 | tf_op jit(solution)/shard_map/stack | solution.py:28
  119.5 12.3 %reverse_select_fusion = bf16[2,2,64,16384]{3,2,1,0:T(8,128)(2,1)} fusion(bf16[2,2,64,16384]{3,2,1,0:T(8,128)(2,1)} %pad_maximum_fusion.1, pred[]{:T(512)S(6)} %eq.67), kind=kLoop, calls=%fused_computation.4 | loop fusion | flops 4194304 | bytes 16777216 | tf_op jit(solution)/shard_map/jit(_where)/select_n | solution.py:31
  131.8 6.9 %collective-permute-start.2 = (bf16[256,16384]{1,0:T(8,128)(2,1)}, bf16[256,16384]{1,0:T(8,128)(2,1)}, u32[]{:S(2)}, u32[]{:S(2)}) collective-permute-start(bf16[256,16384]{1,0:T(8,128)(2,1)} %bitcast.50), channel_id=1, source_target_pairs={{0,4},{4,8},{8,12},{12,16},{16,20},{20,24},{24,28},{1,5},{5,9},{9,... | collective-permute-start | bytes 25165832 | tf_op jit(solution)/shard_map/ppermute | solution.py:40
  138.7 1.3 collective-permute-start.3
  140.0 0.1 fusion.23
  140.0 0.1 reduce_window_sum.18
  140.1 0.2 select_reduce_fusion
  140.3 0.1 fusion.27
  140.4 0.7 all_to_all.12
  141.1 7.0 %all-to-all-start = ((bf16[8,1,16]{2,1,0:T(2,128)(2,1)}), bf16[8,1,16]{2,1,0:T(2,128)(2,1)S(1)}, u32[]{:S(2)}, u32[]{:S(2)}) async-start(bf16[8,1,16]{2,1,0:T(2,128)(2,1)} %all_to_all.12), calls=%async_computation | async-start | bytes 8192 | tf_op jit(solution)/shard_map/all_to_all | solution.py:74
  148.1 3.3 convolution_convert_fusion
  151.4 0.1 copy.50
  151.5 0.1 reshape.96
  151.6 343.1 %all-to-all-done = bf16[8,1,16]{2,1,0:T(2,128)(2,1)S(1)} async-done(((bf16[8,1,16]{2,1,0:T(2,128)(2,1)}), bf16[8,1,16]{2,1,0:T(2,128)(2,1)S(1)}, u32[]{:S(2)}, u32[]{:S(2)}) %all-to-all-start) | async-done | bytes 288 | tf_op jit(solution)/shard_map/all_to_all | solution.py:74
  494.7 6.7 %all-to-all-start.1 = ((bf16[8,16,16384]{2,1,0:T(8,128)(2,1)}), bf16[8,16,16384]{2,1,0:T(8,128)(2,1)}, u32[]{:S(2)}, u32[]{:S(2)}) async-start(bf16[8,16,16384]{2,1,0:T(8,128)(2,1)} %bitcast.54), calls=%async_computation.1 | async-start | bytes 8388608 | tf_op jit(solution)/shard_map/all_to_all | solution.py:67
  501.5 0.5 reduce-scatter.4.cloned.1.call-start
  502.0 5.5 reshape.89
  507.5 2.9 reshape.92
  510.4 0.1 copy.51
  510.5 0.1 copy.53
  510.6 0.1 copy.48
  510.7 17.6 %pad_maximum_fusion = bf16[768,16384]{1,0:T(8,128)(2,1)} fusion(bf16[256,16384]{1,0:T(8,128)(2,1)} %collective-permute-done.3, bf16[256,16384]{1,0:T(8,128)(2,1)} %bitcast.52, bf16[256,16384]{1,0:T(8,128)(2,1)} %collective-permute-done.2), kind=kLoop, calls=%fused_computation.1 | loop fusion | flops 75497472 | bytes 50331648 | tf_op jit(solution)/shard_map/concatenate | solution.py:44
  528.4 22.3 %gather_fusion = bf16[256,16384]{1,0:T(8,128)(2,1)} fusion(bf16[768,16384]{1,0:T(8,128)(2,1)} %pad_maximum_fusion, s32[1024]{0:T(1024)S(1)} %pad_clamp_fusion), kind=kCustom, calls=%fused_computation | custom fusion | bytes 16778240 | tf_op jit(solution)/shard_map/gather | solution.py:99
  550.7 9.4 %copy.62 = bf16[32,8,64,256]{3,2,1,0:T(8,128)(2,1)} copy(bf16[32,8,64,256]{3,1,2,0:T(8,128)(2,1)} %bitcast.48) | data formatting | bytes 16777216
  560.1 6.7 %fusion.12 = bf16[64,64,1,256]{3,1,0,2:T(8,128)(2,1)S(1)} fusion(bf16[64,4,64,256]{3,2,1,0:T(8,128)(2,1)} %bitcast.55, bf16[64,64,4,64]{3,2,1,0:T(4,128)(2,1)} %reshape.89, bf16[64,4]{1,0:T(8,128)(2,1)S(1)} %copy.51), kind=kOutput, calls=%fused_computation.24 | convolution fusion | flops 538968064 | bytes 12583424 | tf_op jit(solution)/shard_map/jake,jkef->jaf/dot_general | solution.py:106
  566.8 0.3 copy-done.1
  567.1 1.2 copy-done.2
  568.3 2.2 fusion.13
  570.6 2.2 fusion.11
  572.8 3.3 pad_maximum_fusion.2
  576.1 12.3 %copy.55 = bf16[64,64,3,256]{3,2,1,0:T(4,128)(2,1)} copy(bf16[64,64,3,256]{3,1,0,2:T(8,128)(2,1)} %pad_maximum_fusion.2) | data formatting | bytes 12582912 | tf_op jit(solution)/shard_map/stack | solution.py:108
  588.4 5.2 copy.63
  593.7 1.8 convolution_bitcast_fusion
  595.5 1.1 copy.60
  596.7 0.1 reshape.108
  596.8 0.1 gt.16
  596.9 0.2 reduce-window.8
  597.1 0.1 add_reduce_fusion
  597.2 4.2 convolution_convert_fusion.1
  601.4 20.0 %reduce-scatter.4.cloned.1.call-done = f32[64,768]{1,0:T(8,128)} async-done(((f32[256,768]{1,0:T(8,128)}), f32[64,768]{1,0:T(8,128)}) %reduce-scatter.4.cloned.1.call-update) | async-done | bytes 196624
  621.4 1.1 copy.61
  622.5 0.8 copy.56
  (19 shorter events, 0.1 us)
Async XLA Ops:
  7.2 4.6 collective-permute-start
  18.0 94.0 %collective-permute-start.1 = (bf16[2,64,16384]{2,1,0:T(8,128)(2,1)}, bf16[2,64,16384]{2,1,0:T(8,128)(2,1)}, u32[]{:S(2)}, u32[]{:S(2)}) collective-permute-start(bf16[2,64,16384]{2,1,0:T(8,128)(2,1)} %get-tuple-element.15), channel_id=1, source_target_pairs={{0,2},{1,3},{2,0},{3,1},{4,6},{5,7},{6,4},{7,5},{8,10},{9,11},{10,... | collective-permute-start | bytes 12582920 | tf_op jit(solution)/shard_map/ppermute | solution.py:27
  119.5 20.5 %copy-start.4 = (s32[64]{0:T(128)S(1)}, s32[64]{0:T(128)}, u32[]{:S(2)}) copy-start(s32[64]{0:T(128)} %param.7) | copy-start | bytes 772
  119.5 28.6 %copy-start.3 = (s32[64,4]{0,1:T(4,128)S(1)}, s32[64,4]{0,1:T(4,128)}, u32[]{:S(2)}) copy-start(s32[64,4]{0,1:T(4,128)} %param.5) | copy-start | bytes 3076
  119.5 28.6 %copy-start = (bf16[64,16384]{1,0:T(8,128)(2,1)S(1)}, bf16[64,16384]{1,0:T(8,128)(2,1)}, u32[]{:S(2)}) copy-start(bf16[64,16384]{1,0:T(8,128)(2,1)} %param.4) | copy-start | bytes 6291460
  131.8 378.9 %collective-permute-start.2 = (bf16[256,16384]{1,0:T(8,128)(2,1)}, bf16[256,16384]{1,0:T(8,128)(2,1)}, u32[]{:S(2)}, u32[]{:S(2)}) collective-permute-start(bf16[256,16384]{1,0:T(8,128)(2,1)} %bitcast.50), channel_id=1, source_target_pairs={{0,4},{4,8},{8,12},{12,16},{16,20},{20,24},{24,28},{1,5},{5,9},{9,... | collective-permute-start | bytes 25165832 | tf_op jit(solution)/shard_map/ppermute | solution.py:40
  138.7 372.1 %collective-permute-start.3 = (bf16[256,16384]{1,0:T(8,128)(2,1)}, bf16[256,16384]{1,0:T(8,128)(2,1)}, u32[]{:S(2)}, u32[]{:S(2)}) collective-permute-start(bf16[256,16384]{1,0:T(8,128)(2,1)} %bitcast.51), channel_id=1, source_target_pairs={{4,0},{8,4},{12,8},{16,12},{20,16},{24,20},{28,24},{5,1},{9,5},{13... | collective-permute-start | bytes 25165832 | tf_op jit(solution)/shard_map/ppermute | solution.py:43
  141.1 353.6 %all-to-all-start = ((bf16[8,1,16]{2,1,0:T(2,128)(2,1)}), bf16[8,1,16]{2,1,0:T(2,128)(2,1)S(1)}, u32[]{:S(2)}, u32[]{:S(2)}) async-start(bf16[8,1,16]{2,1,0:T(2,128)(2,1)} %all_to_all.12), calls=%async_computation | async-start | bytes 8192 | tf_op jit(solution)/shard_map/all_to_all | solution.py:74
  494.7 102.5 %all-to-all-start.1 = ((bf16[8,16,16384]{2,1,0:T(8,128)(2,1)}), bf16[8,16,16384]{2,1,0:T(8,128)(2,1)}, u32[]{:S(2)}, u32[]{:S(2)}) async-start(bf16[8,16,16384]{2,1,0:T(8,128)(2,1)} %bitcast.54), calls=%async_computation.1 | async-start | bytes 8388608 | tf_op jit(solution)/shard_map/all_to_all | solution.py:67
  501.5 120.0 %reduce-scatter.4.cloned.1.call-start = ((), (), s32[]{:S(2)}) async-start(), calls=%async_computation.3 | async-start | bytes 983040
  560.1 7.0 %copy-start.1 = (bf16[32,8,64,256]{3,2,1,0:T(8,128)(2,1)S(1)}, bf16[32,8,64,256]{3,2,1,0:T(8,128)(2,1)}, u32[]{:S(2)}) copy-start(bf16[32,8,64,256]{3,2,1,0:T(8,128)(2,1)} %copy.62) | copy-start | bytes 25165828
  560.1 8.2 %copy-start.2 = (bf16[64,64,4,64]{3,2,1,0:T(4,128)(2,1)S(1)}, bf16[64,64,4,64]{3,2,1,0:T(4,128)(2,1)}, u32[]{:S(2)}) copy-start(bf16[64,64,4,64]{3,2,1,0:T(4,128)(2,1)} %reshape.89) | copy-start | bytes 6291460
Sparse Core Ops, SparseCore 0:
  596.8 24.5 reduce-scatter.3
